TPU v7x, 32 devices: a whole 2x2x4 slice. The times are simulated.
32 devices in a mesh: groups: 2 (over x), rows: 16 (over z, y, core).
Axes of the slice: x: 2, y: 2, z: 4, core: 2. Of those that a mesh axis runs over, the one named last changes fastest.
Arguments:
- token_ids: int32 [1, 256], P(None, 'groups'), parts along dimension 1, may hold values from 0 to 32767
- parents: int32 [1, 8, 32], P(None, 'groups'), parts along dimension 1, may hold values from 0 to 31, as said below
- states: bfloat16 [256, 16, 128, 128], P(('groups', 'rows')), parts along dimension 0, may hold values from -1.75 to 1.75
- embed_table: bfloat16 [32768, 2048], P(None, 'rows'), may hold values from -6 to 6
- qkv_weight: bfloat16 [2048, 3, 2048], P(None, None, 'rows'), may hold values from -0.125 to 0.125
- gate_weight: float32 [16, 128], replicated, may hold values from -6 to 6
- gate_bias: float32 [16], replicated, may hold values from -2 to 3
- norm_gain: float32 [2048], replicated, may hold values from 0.1 to 1.9
- out_weight: bfloat16 [2048, 2048], P(None, 'rows'), may hold values from -0.125 to 0.125
Outputs:
- layer_out: bfloat16 [1, 256, 2048], P(None, 'groups', 'rows'), parts along dimension 1
- final_states: bfloat16 [256, 16, 128, 128], P(('groups', 'rows')), parts along dimension 0
There are 2 independent parts, one for each index of `groups`. A program takes and returns all parts, laid end to end along the dimension named above; an argument that names none is the same for every part. Nothing has to cross between parts.
Inputs may be any that keep to these rules, and one draw needn't show every extreme that they name: The 32 beams of a user fall into 4 aligned blocks of 8. In every step and for every user, at most 2 children of one block have parents in any one other block, and in every step some user has exactly 2 children of one block with parents in another block.
All inputs are finite; a program needn't handle non-finite values.
Results may differ from a plain program's by a relative error of at most 0.0074.
Values may be sent and summed in bfloat16 or wider, within the bound.
A program may use at most 64 MiB of HBM per device.

v0:
```python
import math
import jax
import jax.numpy as jnp
from jax import lax
from jax.sharding import PartitionSpec as P

CAP = 2


def from_partner(block, axis, stride):
    count = lax.axis_size(axis)
    route = []
    for low in range(count):
        high = low | 1 << stride
        if high != low and high < count:
            route += [(low, high), (high, low)]
    return lax.ppermute(block, axis, route)


def outgoing(state_now, parent_list, member, row_local, partner):
    target = jnp.bitwise_xor(member, partner)
    children = lax.dynamic_slice_in_dim(parent_list, target * row_local, row_local, 0)
    needed = children // row_local == member
    rank_index = jnp.cumsum(needed.astype(jnp.int32)) - 1
    slot_ids = jnp.arange(CAP, dtype=jnp.int32)
    chosen = jnp.sum(
        jnp.where(
            needed[None, :] & (rank_index[None, :] == slot_ids[:, None]),
            (children % row_local)[None, :],
            0,
        ),
        axis=1,
    )
    return jnp.take(state_now, chosen, axis=0)


def route(state_now, parent_list, member, row_local):
    first_out = outgoing(state_now, parent_list, member, row_local, 1)
    second_out = outgoing(state_now, parent_list, member, row_local, 2)
    corner_out = outgoing(state_now, parent_list, member, row_local, 3)
    got_one = from_partner(first_out, "rows", 0)
    got_two = from_partner(second_out, "rows", 1)
    relayed = from_partner(corner_out, "rows", 0)
    got_three = from_partner(relayed, "rows", 1)
    own_list = lax.dynamic_slice_in_dim(parent_list, member * row_local, row_local, 0)
    source = own_list // row_local
    partner = jnp.bitwise_xor(source, member)
    slot_index = jnp.arange(row_local, dtype=jnp.int32)
    earlier = (source[:, None] == source[None, :]) & (slot_index[:, None] > slot_index[None, :])
    rank_index = jnp.sum(earlier.astype(jnp.int32), axis=1)
    position = jnp.where(
        partner == 0, own_list % row_local, row_local + (partner - 1) * CAP + rank_index
    )
    pooled = jnp.concatenate([state_now, got_one, got_two, got_three], 0)
    return jnp.take(pooled, position, axis=0)


def per_device(
    token_ids,
    parents,
    states,
    embed_table,
    qkv_weight,
    gate_weight,
    gate_bias,
    norm_gain,
    out_weight,
):
    row_local = states.shape[0]
    heads = states.shape[1]
    head_size = states.shape[2]
    width = heads * head_size
    column_local = embed_table.shape[1]
    row_total = token_ids.shape[1]
    device = lax.axis_index("rows")
    member = device % 4
    user_index = device // 4
    weight_flat = qkv_weight.reshape(qkv_weight.shape[0], 3 * column_local)
    local_columns = jnp.take(embed_table, token_ids, axis=0)
    every_proj = jnp.einsum(
        "...rc,cf->...rf",
        lax.all_gather(local_columns, "rows", axis=2, tiled=True),
        weight_flat,
        preferred_element_type=jnp.float32,
    )
    state_now = states
    step_proj = every_proj[0]
    projected = step_proj.astype(jnp.bfloat16).reshape(row_total, 3, column_local)
    mine = lax.all_to_all(projected, "rows", split_axis=0, concat_axis=2, tiled=True)
    queries = mine[:, 0].reshape(row_local, heads, head_size)
    key_float = mine[:, 1].reshape(row_local, heads, head_size).astype(jnp.float32)
    values = mine[:, 2].reshape(row_local, heads, head_size).astype(jnp.float32)
    gate_logit = jnp.sum(key_float * gate_weight, axis=-1) / math.sqrt(head_size) + gate_bias
    decay_rate = jax.nn.sigmoid(gate_logit)
    key_unit = key_float * lax.rsqrt(jnp.sum(key_float * key_float, axis=-1, keepdims=True) + 1e-06)
    parent_list = lax.dynamic_index_in_dim(parents[0], user_index, 0, keepdims=False)
    prior_state = route(state_now, parent_list, member, row_local)
    new_state = (
        decay_rate[:, :, None, None] * prior_state.astype(jnp.float32)
        + key_unit[:, :, :, None] * values[:, :, None, :]
    )
    state_now = new_state.astype(jnp.bfloat16)
    readout = jnp.einsum("rhd,rhde->rhe", queries, state_now, preferred_element_type=jnp.float32)
    scaled = readout * lax.rsqrt(jnp.mean(readout * readout, axis=-1, keepdims=True) + 1e-05)
    normed = (scaled.reshape(row_local, width) * norm_gain).astype(jnp.bfloat16)
    attention = jnp.dot(
        lax.all_gather(normed, "rows", axis=0, tiled=True),
        out_weight,
        preferred_element_type=jnp.float32,
    )
    outputs = [(local_columns[0].astype(jnp.float32) + attention).astype(jnp.bfloat16)]
    return (jnp.stack(outputs), state_now)


def solution(mesh):
    placed = (
        P(None, "groups"),
        P(None, "groups", None),
        P(("groups", "rows"), None, None, None),
        P(None, "rows"),
        P(None, None, "rows"),
        P(),
        P(),
        P(),
        P(None, "rows"),
    )
    return jax.shard_map(
        per_device,
        mesh=mesh,
        in_specs=placed,
        out_specs=(P(None, "groups", "rows"), P(("groups", "rows"), None, None, None)),
        check_vma=False,
    )
```

profile of v0, /device:TPU:0, one launch (start us, length us, event | category | flops | bytes accessed | tf_op | source)
XLA Modules:
  0.0 127.5 jit_solution(7853263627772895128)
XLA Ops:
  0.7 0.9 compare_convert_fusion.2
  2.0 2.9 %gather_fusion.3 = bf16[2,16,128,128]{3,2,1,0:T(8,128)(2,1)S(1)} fusion(bf16[8,16,128,128]{3,2,1,0:T(8,128)(2,1)} %param.13, s32[1024]{0:T(1024)S(1)} %pad_clamp_fusion.2), kind=kCustom, calls=%fused_computation.1.clone | custom fusion | bytes 2097160 | tf_op jit(solution)/shard_map/jit(_take)/gather | solution.py:34
  4.9 1.1 broadcast_select_fusion.1
  6.1 3.0 %collective-permute-start.1 = (bf16[2,16,128,128]{3,2,1,0:T(8,128)(2,1)}, bf16[2,16,128,128]{3,2,1,0:T(8,128)(2,1)}, u32[]{:S(2)}, u32[]{:S(2)}) collective-permute-start(bf16[2,16,128,128]{3,2,1,0:T(8,128)(2,1)} %broadcast_select_fusion.1), channel_id=1, source_target_pairs={{0,2},{2,0},{1,3},{3,1},{4,6},{6,4},{5,7},{7,5},{8,10},{10,8},{9,1... | collective-permute-start | bytes 3145736 | tf_op jit(solution)/shard_map/ppermute | solution.py:17
  9.4 2.9 %gather_fusion.2 = bf16[2,16,128,128]{3,2,1,0:T(8,128)(2,1)S(1)} fusion(bf16[8,16,128,128]{3,2,1,0:T(8,128)(2,1)} %param.13, s32[1024]{0:T(1024)S(1)} %pad_clamp_fusion.3), kind=kCustom, calls=%fused_computation.clone | custom fusion | bytes 2097160 | tf_op jit(solution)/shard_map/jit(_take)/gather | solution.py:34
  12.4 1.2 broadcast_select_fusion.2
  13.9 2.9 %gather_fusion.4 = bf16[2,16,128,128]{3,2,1,0:T(8,128)(2,1)S(1)} fusion(bf16[8,16,128,128]{3,2,1,0:T(8,128)(2,1)} %param.13, s32[1024]{0:T(1024)S(1)} %pad_clamp_fusion.1), kind=kCustom, calls=%fused_computation.2.clone | custom fusion | bytes 2097160 | tf_op jit(solution)/shard_map/jit(_take)/gather | solution.py:34
  16.9 1.1 broadcast_select_fusion
  18.6 5.1 %gather_fusion = bf16[128,128]{1,0:T(8,128)(2,1)S(1)} fusion(bf16[32768,128]{1,0:T(8,128)(2,1)} %param.14, s32[1024]{0:T(1024)S(1)} %pad_clamp_fusion.4), kind=kCustom, calls=%fused_computation.3 | custom fusion | bytes 66048 | tf_op jit(solution)/shard_map/jit(_take)/gather | solution.py:79
  23.8 26.1 %all_gather.6 = bf16[1,128,2048]{2,1,0:T(8,128)(2,1)S(1)} all-gather(bf16[1,128,128]{2,1,0:T(8,128)(2,1)S(1)} %bitcast_select_fusion), channel_id=1, replica_groups=mesh['groups'=2,'rows'=16] {'rows'}, dimensions={2}, use_global_device_ids=true | all-gather | bytes 557056 | tf_op jit(solution)/shard_map/all_gather | solution.py:82
  49.9 1.7 %copy.31 = bf16[2048,3,128]{0,2,1:T(8,128)(2,1)S(1)} copy(bf16[2048,3,128]{2,0,1:T(8,128)(2,1)} %param.15) | data formatting | bytes 3145728 | tf_op args[4]
  51.6 0.6 fusion.2
  52.2 0.7 copy.32
  52.9 3.5 %all-to-all-start = ((bf16[128,3,128]{2,1,0:T(4,128)(2,1)}), bf16[128,3,128]{2,1,0:T(4,128)(2,1)S(1)}, u32[]{:S(2)}, u32[]{:S(2)}) async-start(bf16[128,3,128]{2,1,0:T(4,128)(2,1)} %copy.32), calls=%async_computation | async-start | bytes 262144 | tf_op jit(solution)/shard_map/all_to_all | solution.py:89
  56.5 0.8 and_select_fusion.15
  57.5 1.9 %collective-permute-start.3 = (bf16[2,16,128,128]{3,2,1,0:T(8,128)(2,1)}, bf16[2,16,128,128]{3,2,1,0:T(8,128)(2,1)S(1)}, u32[]{:S(2)}, u32[]{:S(2)}) collective-permute-start(bf16[2,16,128,128]{3,2,1,0:T(8,128)(2,1)} %collective-permute-done.2), channel_id=1, source_target_pairs={{0,2},{2,0},{1,3},{3,1},{4,6},{6,4},{5,7},{7,5},{8,10},{10,8},{9,1... | collective-permute-start | bytes 3145736 | tf_op jit(solution)/shard_map/ppermute | solution.py:17
  59.3 5.0 %all-to-all-done = bf16[128,3,128]{2,1,0:T(4,128)(2,1)S(1)} async-done(((bf16[128,3,128]{2,1,0:T(4,128)(2,1)}), bf16[128,3,128]{2,1,0:T(4,128)(2,1)S(1)}, u32[]{:S(2)}, u32[]{:S(2)}) %all-to-all-start) | async-done | bytes 98336 | tf_op jit(solution)/shard_map/all_to_all | solution.py:89
  64.8 19.1 %collective-permute-done.3 = bf16[2,16,128,128]{3,2,1,0:T(8,128)(2,1)S(1)} collective-permute-done((bf16[2,16,128,128]{3,2,1,0:T(8,128)(2,1)}, bf16[2,16,128,128]{3,2,1,0:T(8,128)(2,1)S(1)}, u32[]{:S(2)}, u32[]{:S(2)}) %collective-permute-start.3) | collective-permute-done | bytes 1048608 | tf_op jit(solution)/shard_map/ppermute | solution.py:17
  84.0 8.1 %pad_maximum_fusion = bf16[14,16,128,128]{3,2,1,0:T(8,128)(2,1)} fusion(bf16[2,16,128,128]{3,2,1,0:T(8,128)(2,1)S(1)} %collective-permute-done.3, bf16[2,16,128,128]{3,2,1,0:T(8,128)(2,1)} %collective-permute-done.1, bf16[2,16,128,128]{3,2,1,0:T(8,128)(2,1)} %collective-permute-done, bf16[8,16,128,128]{3,2,1,0:T(8,128)(2,1)} %param.13), kind=kLoop, calls=%fused_computation.6 | loop fusion | flops 11010048 | bytes 14680064 | tf_op jit(solution)/shard_map/concatenate | solution.py:54
  92.0 6.2 %gather_fusion.1 = bf16[8,16,128,128]{3,2,1,0:T(8,128)(2,1)} fusion(bf16[14,16,128,128]{3,2,1,0:T(8,128)(2,1)} %pad_maximum_fusion, s32[1024]{0:T(1024)S(1)} %pad_clamp_fusion), kind=kCustom, calls=%fused_computation.4 | custom fusion | bytes 8388640 | tf_op jit(solution)/shard_map/jit(_take)/gather | solution.py:55
  98.2 4.6 %add_convert_fusion = bf16[8,16,128,128]{3,2,1,0:T(8,128)(2,1)S(1)} fusion(f32[8,16,128]{2,1,0:T(8,128)S(1)} %copy.36, f32[8,16,128]{2,1,0:T(8,128)S(1)} %copy.35, bf16[8,16,128,128]{3,2,1,0:T(8,128)(2,1)} %gather_fusion.1, f32[8,16]{1,0:T(8,128)S(1)} %add_divide_fusion, pred[8]{0:T(512)(128)(4,1)S(1)} %compare_and_fusion.3), kind=kLoop, calls=%fused_computation.5 | loop fusion | flops 12582912 | bytes 8520200 | tf_op jit(solution)/shard_map/convert_element_type | solution.py:102
  102.9 1.2 fusion.11
  104.3 22.2 %all_gather.7 = bf16[128,2048]{1,0:T(8,128)(2,1)S(1)} all-gather(bf16[8,2048]{1,0:T(8,128)(2,1)S(1)} %fusion.10), channel_id=1, replica_groups=mesh['groups'=2,'rows'=16] {'rows'}, dimensions={0}, use_global_device_ids=true | all-gather | bytes 557056 | tf_op jit(solution)/shard_map/all_gather | solution.py:107
  126.6 0.9 fusion.6
  (61 shorter events, 2.5 us)
Async XLA Ops:
  0.6 125.9 %copy-start = (bf16[2048,128]{1,0:T(8,128)(2,1)S(1)}, bf16[2048,128]{1,0:T(8,128)(2,1)}, u32[]{:S(2)}) copy-start(bf16[2048,128]{1,0:T(8,128)(2,1)} %param.19) | copy-start | bytes 1572868
  6.1 58.7 %collective-permute-start.1 = (bf16[2,16,128,128]{3,2,1,0:T(8,128)(2,1)}, bf16[2,16,128,128]{3,2,1,0:T(8,128)(2,1)}, u32[]{:S(2)}, u32[]{:S(2)}) collective-permute-start(bf16[2,16,128,128]{3,2,1,0:T(8,128)(2,1)} %broadcast_select_fusion.1), channel_id=1, source_target_pairs={{0,2},{2,0},{1,3},{3,1},{4,6},{6,4},{5,7},{7,5},{8,10},{10,8},{9,1... | collective-permute-start | bytes 3145736 | tf_op jit(solution)/shard_map/ppermute | solution.py:17
  9.4 9.1 %copy-start.5 = (s32[1,128]{1,0:T(1,128)S(1)}, s32[1,128]{1,0:T(1,128)}, u32[]{:S(2)}) copy-start(s32[1,128]{1,0:T(1,128)} %param.11) | copy-start | bytes 1540
  13.6 51.3 %collective-permute-start = (bf16[2,16,128,128]{3,2,1,0:T(8,128)(2,1)}, bf16[2,16,128,128]{3,2,1,0:T(8,128)(2,1)}, u32[]{:S(2)}, u32[]{:S(2)}) collective-permute-start(bf16[2,16,128,128]{3,2,1,0:T(8,128)(2,1)} %broadcast_select_fusion.2), channel_id=1, source_target_pairs={{0,1},{1,0},{2,3},{3,2},{4,5},{5,4},{6,7},{7,6},{8,9},{9,8},{10,11... | collective-permute-start | bytes 3145736 | tf_op jit(solution)/shard_map/ppermute | solution.py:17
  16.9 47.6 %copy-start.2 = (f32[16,128]{1,0:T(8,128)S(1)}, f32[16,128]{1,0:T(8,128)}, u32[]{:S(2)}) copy-start(f32[16,128]{1,0:T(8,128)} %param.16) | copy-start | bytes 24580
  18.0 46.8 %copy-start.4 = (f32[16]{0:T(128)S(1)}, f32[16]{0:T(128)}, u32[]{:S(2)}) copy-start(f32[16]{0:T(128)} %param.17) | copy-start | bytes 196
  18.0 39.4 %collective-permute-start.2 = (bf16[2,16,128,128]{3,2,1,0:T(8,128)(2,1)}, bf16[2,16,128,128]{3,2,1,0:T(8,128)(2,1)}, u32[]{:S(2)}, u32[]{:S(2)}) collective-permute-start(bf16[2,16,128,128]{3,2,1,0:T(8,128)(2,1)} %broadcast_select_fusion), channel_id=1, source_target_pairs={{0,1},{1,0},{2,3},{3,2},{4,5},{5,4},{6,7},{7,6},{8,9},{9,8},{10,11... | collective-permute-start | bytes 3145736 | tf_op jit(solution)/shard_map/ppermute | solution.py:17
  52.9 11.4 %all-to-all-start = ((bf16[128,3,128]{2,1,0:T(4,128)(2,1)}), bf16[128,3,128]{2,1,0:T(4,128)(2,1)S(1)}, u32[]{:S(2)}, u32[]{:S(2)}) async-start(bf16[128,3,128]{2,1,0:T(4,128)(2,1)} %copy.32), calls=%async_computation | async-start | bytes 262144 | tf_op jit(solution)/shard_map/all_to_all | solution.py:89
  57.5 26.5 %collective-permute-start.3 = (bf16[2,16,128,128]{3,2,1,0:T(8,128)(2,1)}, bf16[2,16,128,128]{3,2,1,0:T(8,128)(2,1)S(1)}, u32[]{:S(2)}, u32[]{:S(2)}) collective-permute-start(bf16[2,16,128,128]{3,2,1,0:T(8,128)(2,1)} %collective-permute-done.2), channel_id=1, source_target_pairs={{0,2},{2,0},{1,3},{3,1},{4,6},{6,4},{5,7},{7,5},{8,10},{10,8},{9,1... | collective-permute-start | bytes 3145736 | tf_op jit(solution)/shard_map/ppermute | solution.py:17
  102.9 24.6 %copy-start.1 = (bf16[8,16,128,128]{3,2,1,0:T(8,128)(2,1)}, bf16[8,16,128,128]{3,2,1,0:T(8,128)(2,1)S(1)}, u32[]{:S(2)}) copy-start(bf16[8,16,128,128]{3,2,1,0:T(8,128)(2,1)S(1)} %add_convert_fusion) | copy-start | bytes 12582916
  102.9 1.4 %copy-start.3 = (f32[2048]{0:T(1024)S(1)}, f32[2048]{0:T(1024)}, u32[]{:S(2)}) copy-start(f32[2048]{0:T(1024)} %param.18) | copy-start | bytes 24580
where the time goes:
time: 128 us; the launch traced here: 127 us
  blocking collectives  48.4 us (38%)
  waiting for transfers between devices  24.1 us (19%)
  local copies, waits for them, and re-layouts  22.8 us (18%)
  other arithmetic  19.6 us (15%)
  starting transfers between devices  8.87 us (7%)
  matrix products  2.7 us (2%)
    all_gather x1, blocking collectives, per_device(): lax.all_gather(local_columns, 'rows', axis=2, tiled=True)  26.1 us
    all_gather x1, blocking collectives, per_device(): lax.all_gather(normed, 'rows', axis=0, tiled=True)  22.2 us
    ppermute x4, waiting for transfers between devices, from_partner(): return lax.ppermute(block, axis, route)  19.2 us
    gather x3, local copies, waits for them, and re-layouts, outgoing(): return jnp.take(state_now, chosen, axis=0)  8.82 us
    concatenate x1, other arithmetic, route(): pooled = jnp.concatenate([state_now, got_one, got_two, got_three], 0)  8.06 us
    gather x1, local copies, waits for them, and re-layouts, route(): return jnp.take(pooled, position, axis=0)  6.18 us
    ppermute x4, starting transfers between devices, from_partner(): return lax.ppermute(block, axis, route)  5.36 us
    gather x1, local copies, waits for them, and re-layouts, per_device(): local_columns = jnp.take(embed_table, token_ids, axis=0)  5.11 us
  transfers between devices with their start and end apart: 5, of which 2 were waited for; matrix products, arithmetic and copies ran while one was open for 15% of the time, Pallas kernels for 0%

commit v1 on v0

--- a/solution.py
+++ b/solution.py
@@ -103,11 +103,28 @@
     readout = jnp.einsum("rhd,rhde->rhe", queries, state_now, preferred_element_type=jnp.float32)
     scaled = readout * lax.rsqrt(jnp.mean(readout * readout, axis=-1, keepdims=True) + 1e-05)
     normed = (scaled.reshape(row_local, width) * norm_gain).astype(jnp.bfloat16)
-    attention = jnp.dot(
-        lax.all_gather(normed, "rows", axis=0, tiled=True),
-        out_weight,
-        preferred_element_type=jnp.float32,
-    )
+
+    def state_obtain(unit):
+        work_now, z1, small = (lax.axis_size("rows"), lax.axis_index("rows"), unit.shape[0])
+        log = tuple(((k, (k + 1) % work_now) for k in range(work_now)))
+        kept_rows = tuple(((k, (k - 1) % work_now) for k in range(work_now)))
+        u_next = jnp.zeros((*unit.shape[:0], work_now * small, *unit.shape[1:]), unit.dtype)
+        u_next = lax.dynamic_update_slice_in_dim(u_next, unit, z1 * small, axis=0)
+        now = near = unit
+        new = work_now // 2
+        for at in range(1, new + 1):
+            now = lax.ppermute(now, perm=log, axis_name="rows")
+            u_next = lax.dynamic_update_slice_in_dim(
+                u_next, now, (z1 - at) % work_now * small, axis=0
+            )
+            if at < work_now - new:
+                near = lax.ppermute(near, perm=kept_rows, axis_name="rows")
+                u_next = lax.dynamic_update_slice_in_dim(
+                    u_next, near, (z1 + at) % work_now * small, axis=0
+                )
+        return u_next
+
+    attention = jnp.dot(state_obtain(normed), out_weight, preferred_element_type=jnp.float32)
     outputs = [(local_columns[0].astype(jnp.float32) + attention).astype(jnp.bfloat16)]
     return (jnp.stack(outputs), state_now)
 

time: 128 us -> 156 us (1.22)
  starting transfers between devices: 8.87 us -> 40 us
  blocking collectives: 48.4 us -> 26.1 us
  waiting for transfers between devices: 24.1 us -> 41.3 us
  local copies, waits for them, and re-layouts: 22.8 us -> 24.9 us
    ppermute x0 -> x15, starting transfers between devices: none -> 31.1 us  [the longest x7 31.1 us: state_obtain(): near = lax.ppermute(near, perm=kept_rows, axis_name='rows')]
    all_gather x1 -> x0, blocking collectives: 22.2 us -> none  [per_device(): lax.all_gather(normed, 'rows', axis=0, tiled=True)]
    ppermute x0 -> x15, waiting for transfers between devices: none -> 17.2 us  [the longest x8 17.2 us: state_obtain(): now = lax.ppermute(now, perm=log, axis_name='rows')]
    unnamed x13, local copies, waits for them, and re-layouts: 1.76 us -> 3.75 us
  transfers between devices with their start and end apart: 5 -> 20, of which waited for: 2 -> 10; matrix products, arithmetic and copies ran while one was open for 15% -> 12% of each run, Pallas kernels for 0% -> 0%
where the time goes in v1:
time: 156 us
  waiting for transfers between devices  41.3 us (26%)
  starting transfers between devices  40 us (26%)
  blocking collectives  26.1 us (17%)
  local copies, waits for them, and re-layouts  24.9 us (16%)
  other arithmetic  19.6 us (13%)
  matrix products  2.69 us (2%)
    ppermute x7, starting transfers between devices, state_obtain(): near = lax.ppermute(near, perm=kept_rows, axis_name='rows')  31.1 us
    all_gather x1, blocking collectives, per_device(): lax.all_gather(local_columns, 'rows', axis=2, tiled=True)  26.1 us
    ppermute x4, waiting for transfers between devices, from_partner(): return lax.ppermute(block, axis, route)  19.2 us
    ppermute x8, waiting for transfers between devices, state_obtain(): now = lax.ppermute(now, perm=log, axis_name='rows')  17.2 us
    gather x3, local copies, waits for them, and re-layouts, outgoing(): return jnp.take(state_now, chosen, axis=0)  8.82 us
    concatenate x1, other arithmetic, route(): pooled = jnp.concatenate([state_now, got_one, got_two, got_three], 0)  8.11 us
    gather x1, local copies, waits for them, and re-layouts, route(): return jnp.take(pooled, position, axis=0)  6.18 us
    ppermute x4, starting transfers between devices, from_partner(): return lax.ppermute(block, axis, route)  5.36 us
  transfers between devices with their start and end apart: 20, of which 10 were waited for; matrix products, arithmetic and copies ran while one was open for 12% of the time, Pallas kernels for 0%

profile of v1, /device:TPU:0, one launch (start us, length us, event | category | flops | bytes accessed | tf_op | source)
XLA Modules:
  0.0 155.8 jit_solution(16505819087544585587)
XLA Ops:
  2.0 2.9 %gather_fusion.3 = bf16[2,16,128,128]{3,2,1,0:T(8,128)(2,1)S(1)} fusion(bf16[8,16,128,128]{3,2,1,0:T(8,128)(2,1)} %param.13, s32[1024]{0:T(1024)S(1)} %pad_clamp_fusion.2), kind=kCustom, calls=%fused_computation.1.clone | custom fusion | bytes 2097160 | tf_op jit(solution)/shard_map/jit(_take)/gather | solution.py:34
  6.0 3.0 %collective-permute-start.1 = (bf16[2,16,128,128]{3,2,1,0:T(8,128)(2,1)}, bf16[2,16,128,128]{3,2,1,0:T(8,128)(2,1)}, u32[]{:S(2)}, u32[]{:S(2)}) collective-permute-start(bf16[2,16,128,128]{3,2,1,0:T(8,128)(2,1)} %broadcast_select_fusion.1), channel_id=1, source_target_pairs={{0,2},{2,0},{1,3},{3,1},{4,6},{6,4},{5,7},{7,5},{8,10},{10,8},{9,1... | collective-permute-start | bytes 3145736 | tf_op jit(solution)/shard_map/ppermute | solution.py:17
  9.4 2.9 %gather_fusion.2 = bf16[2,16,128,128]{3,2,1,0:T(8,128)(2,1)S(1)} fusion(bf16[8,16,128,128]{3,2,1,0:T(8,128)(2,1)} %param.13, s32[1024]{0:T(1024)S(1)} %pad_clamp_fusion.3), kind=kCustom, calls=%fused_computation.clone | custom fusion | bytes 2097160 | tf_op jit(solution)/shard_map/jit(_take)/gather | solution.py:34
  13.9 2.9 %gather_fusion.4 = bf16[2,16,128,128]{3,2,1,0:T(8,128)(2,1)S(1)} fusion(bf16[8,16,128,128]{3,2,1,0:T(8,128)(2,1)} %param.13, s32[1024]{0:T(1024)S(1)} %pad_clamp_fusion.1), kind=kCustom, calls=%fused_computation.2.clone | custom fusion | bytes 2097160 | tf_op jit(solution)/shard_map/jit(_take)/gather | solution.py:34
  18.5 5.1 %gather_fusion = bf16[128,128]{1,0:T(8,128)(2,1)S(1)} fusion(bf16[32768,128]{1,0:T(8,128)(2,1)} %param.14, s32[1024]{0:T(1024)S(1)} %pad_clamp_fusion.4), kind=kCustom, calls=%fused_computation.3 | custom fusion | bytes 66048 | tf_op jit(solution)/shard_map/jit(_take)/gather | solution.py:79
  23.7 26.1 %all_gather.3 = bf16[1,128,2048]{2,1,0:T(8,128)(2,1)S(1)} all-gather(bf16[1,128,128]{2,1,0:T(8,128)(2,1)S(1)} %bitcast_select_fusion), channel_id=1, replica_groups=mesh['groups'=2,'rows'=16] {'rows'}, dimensions={2}, use_global_device_ids=true | all-gather | bytes 557056 | tf_op jit(solution)/shard_map/all_gather | solution.py:82
  49.9 1.7 %copy.31 = bf16[2048,3,128]{0,2,1:T(8,128)(2,1)S(1)} copy(bf16[2048,3,128]{2,0,1:T(8,128)(2,1)} %param.15) | data formatting | bytes 3145728 | tf_op args[4]
  52.9 3.5 %all-to-all-start = ((bf16[128,3,128]{2,1,0:T(4,128)(2,1)}), bf16[128,3,128]{2,1,0:T(4,128)(2,1)S(1)}, u32[]{:S(2)}, u32[]{:S(2)}) async-start(bf16[128,3,128]{2,1,0:T(4,128)(2,1)} %copy.32), calls=%async_computation | async-start | bytes 262144 | tf_op jit(solution)/shard_map/all_to_all | solution.py:89
  57.5 1.9 %collective-permute-start.3 = (bf16[2,16,128,128]{3,2,1,0:T(8,128)(2,1)}, bf16[2,16,128,128]{3,2,1,0:T(8,128)(2,1)S(1)}, u32[]{:S(2)}, u32[]{:S(2)}) collective-permute-start(bf16[2,16,128,128]{3,2,1,0:T(8,128)(2,1)} %collective-permute-done.2), channel_id=1, source_target_pairs={{0,2},{2,0},{1,3},{3,1},{4,6},{6,4},{5,7},{7,5},{8,10},{10,8},{9,1... | collective-permute-start | bytes 3145736 | tf_op jit(solution)/shard_map/ppermute | solution.py:17
  59.3 5.0 %all-to-all-done = bf16[128,3,128]{2,1,0:T(4,128)(2,1)S(1)} async-done(((bf16[128,3,128]{2,1,0:T(4,128)(2,1)}), bf16[128,3,128]{2,1,0:T(4,128)(2,1)S(1)}, u32[]{:S(2)}, u32[]{:S(2)}) %all-to-all-start) | async-done | bytes 98336 | tf_op jit(solution)/shard_map/all_to_all | solution.py:89
  64.8 19.1 %collective-permute-done.3 = bf16[2,16,128,128]{3,2,1,0:T(8,128)(2,1)S(1)} collective-permute-done((bf16[2,16,128,128]{3,2,1,0:T(8,128)(2,1)}, bf16[2,16,128,128]{3,2,1,0:T(8,128)(2,1)S(1)}, u32[]{:S(2)}, u32[]{:S(2)}) %collective-permute-start.3) | collective-permute-done | bytes 1048608 | tf_op jit(solution)/shard_map/ppermute | solution.py:17
  84.0 8.1 %pad_maximum_fusion = bf16[14,16,128,128]{3,2,1,0:T(8,128)(2,1)} fusion(bf16[2,16,128,128]{3,2,1,0:T(8,128)(2,1)S(1)} %collective-permute-done.3, bf16[2,16,128,128]{3,2,1,0:T(8,128)(2,1)} %collective-permute-done.1, bf16[2,16,128,128]{3,2,1,0:T(8,128)(2,1)} %collective-permute-done, bf16[8,16,128,128]{3,2,1,0:T(8,128)(2,1)} %param.13), kind=kLoop, calls=%fused_computation.6 | loop fusion | flops 11010048 | bytes 14680064 | tf_op jit(solution)/shard_map/concatenate | solution.py:54
  92.1 6.2 %gather_fusion.1 = bf16[8,16,128,128]{3,2,1,0:T(8,128)(2,1)} fusion(bf16[14,16,128,128]{3,2,1,0:T(8,128)(2,1)} %pad_maximum_fusion, s32[1024]{0:T(1024)S(1)} %pad_clamp_fusion), kind=kCustom, calls=%fused_computation.4 | custom fusion | bytes 8388640 | tf_op jit(solution)/shard_map/jit(_take)/gather | solution.py:55
  98.3 4.6 %add_convert_fusion = bf16[8,16,128,128]{3,2,1,0:T(8,128)(2,1)S(1)} fusion(f32[8,16,128]{2,1,0:T(8,128)S(1)} %copy.36, f32[8,16,128]{2,1,0:T(8,128)S(1)} %copy.35, bf16[8,16,128,128]{3,2,1,0:T(8,128)(2,1)} %gather_fusion.1, f32[8,16]{1,0:T(8,128)S(1)} %add_divide_fusion, pred[8]{0:T(512)(128)(4,1)S(1)} %compare_and_fusion.3), kind=kLoop, calls=%fused_computation.5 | loop fusion | flops 12582912 | bytes 8520200 | tf_op jit(solution)/shard_map/convert_element_type | solution.py:102
  102.9 2.0 %copy-done.1 = bf16[8,16,128,128]{3,2,1,0:T(8,128)(2,1)} copy-done((bf16[8,16,128,128]{3,2,1,0:T(8,128)(2,1)}, bf16[8,16,128,128]{3,2,1,0:T(8,128)(2,1)S(1)}, u32[]{:S(2)}) %copy-start.1) | copy-done | bytes 4194328
  106.5 4.4 %collective-permute-start.5 = (bf16[8,2048]{1,0:T(8,128)(2,1)S(1)}, bf16[8,2048]{1,0:T(8,128)(2,1)S(1)}, u32[]{:S(2)}, u32[]{:S(2)}) collective-permute-start(bf16[8,2048]{1,0:T(8,128)(2,1)S(1)} %get-tuple-element.6), channel_id=1, source_target_pairs={{0,15},{1,0},{2,1},{3,2},{4,3},{5,4},{6,5},{7,6},{8,7},{9,8},{10,9... | collective-permute-start | bytes 98312 | tf_op jit(solution)/shard_map/ppermute | solution.py:121
  112.5 4.4 %collective-permute-start.7 = (bf16[8,2048]{1,0:T(8,128)(2,1)S(1)}, bf16[8,2048]{1,0:T(8,128)(2,1)S(1)}, u32[]{:S(2)}, u32[]{:S(2)}) collective-permute-start(bf16[8,2048]{1,0:T(8,128)(2,1)S(1)} %collective-permute-done.5), channel_id=1, source_target_pairs={{0,15},{1,0},{2,1},{3,2},{4,3},{5,4},{6,5},{7,6},{8,7},{9,8},{10,9... | collective-permute-start | bytes 98312 | tf_op jit(solution)/shard_map/ppermute | solution.py:121
  116.9 1.7 %collective-permute-done.6 = bf16[8,2048]{1,0:T(8,128)(2,1)S(1)} collective-permute-done((bf16[8,2048]{1,0:T(8,128)(2,1)S(1)}, bf16[8,2048]{1,0:T(8,128)(2,1)S(1)}, u32[]{:S(2)}, u32[]{:S(2)}) %collective-permute-start.6) | collective-permute-done | bytes 32800 | tf_op jit(solution)/shard_map/ppermute | solution.py:116
  118.6 4.4 %collective-permute-start.9 = (bf16[8,2048]{1,0:T(8,128)(2,1)S(1)}, bf16[8,2048]{1,0:T(8,128)(2,1)S(1)}, u32[]{:S(2)}, u32[]{:S(2)}) collective-permute-start(bf16[8,2048]{1,0:T(8,128)(2,1)S(1)} %collective-permute-done.7), channel_id=1, source_target_pairs={{0,15},{1,0},{2,1},{3,2},{4,3},{5,4},{6,5},{7,6},{8,7},{9,8},{10,9... | collective-permute-start | bytes 98312 | tf_op jit(solution)/shard_map/ppermute | solution.py:121
  124.7 4.4 %collective-permute-start.11 = (bf16[8,2048]{1,0:T(8,128)(2,1)S(1)}, bf16[8,2048]{1,0:T(8,128)(2,1)S(1)}, u32[]{:S(2)}, u32[]{:S(2)}) collective-permute-start(bf16[8,2048]{1,0:T(8,128)(2,1)S(1)} %collective-permute-done.9), channel_id=1, source_target_pairs={{0,15},{1,0},{2,1},{3,2},{4,3},{5,4},{6,5},{7,6},{8,7},{9,8},{10,9... | collective-permute-start | bytes 98312 | tf_op jit(solution)/shard_map/ppermute | solution.py:121
  130.7 4.4 %collective-permute-start.13 = (bf16[8,2048]{1,0:T(8,128)(2,1)S(1)}, bf16[8,2048]{1,0:T(8,128)(2,1)S(1)}, u32[]{:S(2)}, u32[]{:S(2)}) collective-permute-start(bf16[8,2048]{1,0:T(8,128)(2,1)S(1)} %collective-permute-done.11), channel_id=1, source_target_pairs={{0,15},{1,0},{2,1},{3,2},{4,3},{5,4},{6,5},{7,6},{8,7},{9,8},{10,9... | collective-permute-start | bytes 98312 | tf_op jit(solution)/shard_map/ppermute | solution.py:121
  136.7 4.4 %collective-permute-start.15 = (bf16[8,2048]{1,0:T(8,128)(2,1)S(1)}, bf16[8,2048]{1,0:T(8,128)(2,1)S(1)}, u32[]{:S(2)}, u32[]{:S(2)}) collective-permute-start(bf16[8,2048]{1,0:T(8,128)(2,1)S(1)} %collective-permute-done.13), channel_id=1, source_target_pairs={{0,15},{1,0},{2,1},{3,2},{4,3},{5,4},{6,5},{7,6},{8,7},{9,8},{10,9... | collective-permute-start | bytes 98312 | tf_op jit(solution)/shard_map/ppermute | solution.py:121
  142.8 4.4 %collective-permute-start.17 = (bf16[8,2048]{1,0:T(8,128)(2,1)S(1)}, bf16[8,2048]{1,0:T(8,128)(2,1)S(1)}, u32[]{:S(2)}, u32[]{:S(2)}) collective-permute-start(bf16[8,2048]{1,0:T(8,128)(2,1)S(1)} %collective-permute-done.15), channel_id=1, source_target_pairs={{0,15},{1,0},{2,1},{3,2},{4,3},{5,4},{6,5},{7,6},{8,7},{9,8},{10,9... | collective-permute-start | bytes 98312 | tf_op jit(solution)/shard_map/ppermute | solution.py:121
  148.8 6.0 %collective-permute-done.18 = bf16[8,2048]{1,0:T(8,128)(2,1)S(1)} collective-permute-done((bf16[8,2048]{1,0:T(8,128)(2,1)S(1)}, bf16[8,2048]{1,0:T(8,128)(2,1)S(1)}, u32[]{:S(2)}, u32[]{:S(2)}) %collective-permute-start.18) | collective-permute-done | bytes 32800 | tf_op jit(solution)/shard_map/ppermute | solution.py:116
  (105 shorter events, 20.7 us)
Async XLA Ops:
  0.6 154.2 %copy-start = (bf16[2048,128]{1,0:T(8,128)(2,1)S(1)}, bf16[2048,128]{1,0:T(8,128)(2,1)}, u32[]{:S(2)}) copy-start(bf16[2048,128]{1,0:T(8,128)(2,1)} %param.19) | copy-start | bytes 1572868
  6.0 58.8 %collective-permute-start.1 = (bf16[2,16,128,128]{3,2,1,0:T(8,128)(2,1)}, bf16[2,16,128,128]{3,2,1,0:T(8,128)(2,1)}, u32[]{:S(2)}, u32[]{:S(2)}) collective-permute-start(bf16[2,16,128,128]{3,2,1,0:T(8,128)(2,1)} %broadcast_select_fusion.1), channel_id=1, source_target_pairs={{0,2},{2,0},{1,3},{3,1},{4,6},{6,4},{5,7},{7,5},{8,10},{10,8},{9,1... | collective-permute-start | bytes 3145736 | tf_op jit(solution)/shard_map/ppermute | solution.py:17
  9.4 9.1 %copy-start.5 = (s32[1,128]{1,0:T(1,128)S(1)}, s32[1,128]{1,0:T(1,128)}, u32[]{:S(2)}) copy-start(s32[1,128]{1,0:T(1,128)} %param.11) | copy-start | bytes 1540
  13.5 51.3 %collective-permute-start = (bf16[2,16,128,128]{3,2,1,0:T(8,128)(2,1)}, bf16[2,16,128,128]{3,2,1,0:T(8,128)(2,1)}, u32[]{:S(2)}, u32[]{:S(2)}) collective-permute-start(bf16[2,16,128,128]{3,2,1,0:T(8,128)(2,1)} %broadcast_select_fusion.2), channel_id=1, source_target_pairs={{0,1},{1,0},{2,3},{3,2},{4,5},{5,4},{6,7},{7,6},{8,9},{9,8},{10,11... | collective-permute-start | bytes 3145736 | tf_op jit(solution)/shard_map/ppermute | solution.py:17
  16.8 47.6 %copy-start.2 = (f32[16,128]{1,0:T(8,128)S(1)}, f32[16,128]{1,0:T(8,128)}, u32[]{:S(2)}) copy-start(f32[16,128]{1,0:T(8,128)} %param.16) | copy-start | bytes 24580
  18.0 46.8 %copy-start.4 = (f32[16]{0:T(128)S(1)}, f32[16]{0:T(128)}, u32[]{:S(2)}) copy-start(f32[16]{0:T(128)} %param.17) | copy-start | bytes 196
  18.0 39.5 %collective-permute-start.2 = (bf16[2,16,128,128]{3,2,1,0:T(8,128)(2,1)}, bf16[2,16,128,128]{3,2,1,0:T(8,128)(2,1)}, u32[]{:S(2)}, u32[]{:S(2)}) collective-permute-start(bf16[2,16,128,128]{3,2,1,0:T(8,128)(2,1)} %broadcast_select_fusion), channel_id=1, source_target_pairs={{0,1},{1,0},{2,3},{3,2},{4,5},{5,4},{6,7},{7,6},{8,9},{9,8},{10,11... | collective-permute-start | bytes 3145736 | tf_op jit(solution)/shard_map/ppermute | solution.py:17
  52.9 11.4 %all-to-all-start = ((bf16[128,3,128]{2,1,0:T(4,128)(2,1)}), bf16[128,3,128]{2,1,0:T(4,128)(2,1)S(1)}, u32[]{:S(2)}, u32[]{:S(2)}) async-start(bf16[128,3,128]{2,1,0:T(4,128)(2,1)} %copy.32), calls=%async_computation | async-start | bytes 262144 | tf_op jit(solution)/shard_map/all_to_all | solution.py:89
  57.5 26.5 %collective-permute-start.3 = (bf16[2,16,128,128]{3,2,1,0:T(8,128)(2,1)}, bf16[2,16,128,128]{3,2,1,0:T(8,128)(2,1)S(1)}, u32[]{:S(2)}, u32[]{:S(2)}) collective-permute-start(bf16[2,16,128,128]{3,2,1,0:T(8,128)(2,1)} %collective-permute-done.2), channel_id=1, source_target_pairs={{0,2},{2,0},{1,3},{3,1},{4,6},{6,4},{5,7},{7,5},{8,10},{10,8},{9,1... | collective-permute-start | bytes 3145736 | tf_op jit(solution)/shard_map/ppermute | solution.py:17
  106.4 6.1 %collective-permute-start.4 = (bf16[8,2048]{1,0:T(8,128)(2,1)S(1)}, bf16[8,2048]{1,0:T(8,128)(2,1)S(1)}, u32[]{:S(2)}, u32[]{:S(2)}) collective-permute-start(bf16[8,2048]{1,0:T(8,128)(2,1)S(1)} %get-tuple-element.6), channel_id=1, source_target_pairs={{0,1},{1,2},{2,3},{3,4},{4,5},{5,6},{6,7},{7,8},{8,9},{9,10},{10,1... | collective-permute-start | bytes 98312 | tf_op jit(solution)/shard_map/ppermute | solution.py:116
  106.5 6.0 %collective-permute-start.5 = (bf16[8,2048]{1,0:T(8,128)(2,1)S(1)}, bf16[8,2048]{1,0:T(8,128)(2,1)S(1)}, u32[]{:S(2)}, u32[]{:S(2)}) collective-permute-start(bf16[8,2048]{1,0:T(8,128)(2,1)S(1)} %get-tuple-element.6), channel_id=1, source_target_pairs={{0,15},{1,0},{2,1},{3,2},{4,3},{5,4},{6,5},{7,6},{8,7},{9,8},{10,9... | collective-permute-start | bytes 98312 | tf_op jit(solution)/shard_map/ppermute | solution.py:121
  112.5 6.1 %collective-permute-start.6 = (bf16[8,2048]{1,0:T(8,128)(2,1)S(1)}, bf16[8,2048]{1,0:T(8,128)(2,1)S(1)}, u32[]{:S(2)}, u32[]{:S(2)}) collective-permute-start(bf16[8,2048]{1,0:T(8,128)(2,1)S(1)} %collective-permute-done.4), channel_id=1, source_target_pairs={{0,1},{1,2},{2,3},{3,4},{4,5},{5,6},{6,7},{7,8},{8,9},{9,10},{10,1... | collective-permute-start | bytes 98312 | tf_op jit(solution)/shard_map/ppermute | solution.py:116
  112.5 6.1 %collective-permute-start.7 = (bf16[8,2048]{1,0:T(8,128)(2,1)S(1)}, bf16[8,2048]{1,0:T(8,128)(2,1)S(1)}, u32[]{:S(2)}, u32[]{:S(2)}) collective-permute-start(bf16[8,2048]{1,0:T(8,128)(2,1)S(1)} %collective-permute-done.5), channel_id=1, source_target_pairs={{0,15},{1,0},{2,1},{3,2},{4,3},{5,4},{6,5},{7,6},{8,7},{9,8},{10,9... | collective-permute-start | bytes 98312 | tf_op jit(solution)/shard_map/ppermute | solution.py:121
  118.6 6.0 %collective-permute-start.8 = (bf16[8,2048]{1,0:T(8,128)(2,1)S(1)}, bf16[8,2048]{1,0:T(8,128)(2,1)S(1)}, u32[]{:S(2)}, u32[]{:S(2)}) collective-permute-start(bf16[8,2048]{1,0:T(8,128)(2,1)S(1)} %collective-permute-done.6), channel_id=1, source_target_pairs={{0,1},{1,2},{2,3},{3,4},{4,5},{5,6},{6,7},{7,8},{8,9},{9,10},{10,1... | collective-permute-start | bytes 98312 | tf_op jit(solution)/shard_map/ppermute | solution.py:116
  118.6 6.0 %collective-permute-start.9 = (bf16[8,2048]{1,0:T(8,128)(2,1)S(1)}, bf16[8,2048]{1,0:T(8,128)(2,1)S(1)}, u32[]{:S(2)}, u32[]{:S(2)}) collective-permute-start(bf16[8,2048]{1,0:T(8,128)(2,1)S(1)} %collective-permute-done.7), channel_id=1, source_target_pairs={{0,15},{1,0},{2,1},{3,2},{4,3},{5,4},{6,5},{7,6},{8,7},{9,8},{10,9... | collective-permute-start | bytes 98312 | tf_op jit(solution)/shard_map/ppermute | solution.py:121
  124.7 6.0 %collective-permute-start.10 = (bf16[8,2048]{1,0:T(8,128)(2,1)S(1)}, bf16[8,2048]{1,0:T(8,128)(2,1)S(1)}, u32[]{:S(2)}, u32[]{:S(2)}) collective-permute-start(bf16[8,2048]{1,0:T(8,128)(2,1)S(1)} %collective-permute-done.8), channel_id=1, source_target_pairs={{0,1},{1,2},{2,3},{3,4},{4,5},{5,6},{6,7},{7,8},{8,9},{9,10},{10,1... | collective-permute-start | bytes 98312 | tf_op jit(solution)/shard_map/ppermute | solution.py:116
  124.7 6.0 %collective-permute-start.11 = (bf16[8,2048]{1,0:T(8,128)(2,1)S(1)}, bf16[8,2048]{1,0:T(8,128)(2,1)S(1)}, u32[]{:S(2)}, u32[]{:S(2)}) collective-permute-start(bf16[8,2048]{1,0:T(8,128)(2,1)S(1)} %collective-permute-done.9), channel_id=1, source_target_pairs={{0,15},{1,0},{2,1},{3,2},{4,3},{5,4},{6,5},{7,6},{8,7},{9,8},{10,9... | collective-permute-start | bytes 98312 | tf_op jit(solution)/shard_map/ppermute | solution.py:121
  130.7 6.0 %collective-permute-start.12 = (bf16[8,2048]{1,0:T(8,128)(2,1)S(1)}, bf16[8,2048]{1,0:T(8,128)(2,1)S(1)}, u32[]{:S(2)}, u32[]{:S(2)}) collective-permute-start(bf16[8,2048]{1,0:T(8,128)(2,1)S(1)} %collective-permute-done.10), channel_id=1, source_target_pairs={{0,1},{1,2},{2,3},{3,4},{4,5},{5,6},{6,7},{7,8},{8,9},{9,10},{10,1... | collective-permute-start | bytes 98312 | tf_op jit(solution)/shard_map/ppermute | solution.py:116
  130.7 6.0 %collective-permute-start.13 = (bf16[8,2048]{1,0:T(8,128)(2,1)S(1)}, bf16[8,2048]{1,0:T(8,128)(2,1)S(1)}, u32[]{:S(2)}, u32[]{:S(2)}) collective-permute-start(bf16[8,2048]{1,0:T(8,128)(2,1)S(1)} %collective-permute-done.11), channel_id=1, source_target_pairs={{0,15},{1,0},{2,1},{3,2},{4,3},{5,4},{6,5},{7,6},{8,7},{9,8},{10,9... | collective-permute-start | bytes 98312 | tf_op jit(solution)/shard_map/ppermute | solution.py:121
  136.7 6.0 %collective-permute-start.14 = (bf16[8,2048]{1,0:T(8,128)(2,1)S(1)}, bf16[8,2048]{1,0:T(8,128)(2,1)S(1)}, u32[]{:S(2)}, u32[]{:S(2)}) collective-permute-start(bf16[8,2048]{1,0:T(8,128)(2,1)S(1)} %collective-permute-done.12), channel_id=1, source_target_pairs={{0,1},{1,2},{2,3},{3,4},{4,5},{5,6},{6,7},{7,8},{8,9},{9,10},{10,1... | collective-permute-start | bytes 98312 | tf_op jit(solution)/shard_map/ppermute | solution.py:116
  136.7 6.0 %collective-permute-start.15 = (bf16[8,2048]{1,0:T(8,128)(2,1)S(1)}, bf16[8,2048]{1,0:T(8,128)(2,1)S(1)}, u32[]{:S(2)}, u32[]{:S(2)}) collective-permute-start(bf16[8,2048]{1,0:T(8,128)(2,1)S(1)} %collective-permute-done.13), channel_id=1, source_target_pairs={{0,15},{1,0},{2,1},{3,2},{4,3},{5,4},{6,5},{7,6},{8,7},{9,8},{10,9... | collective-permute-start | bytes 98312 | tf_op jit(solution)/shard_map/ppermute | solution.py:121
  142.8 6.0 %collective-permute-start.16 = (bf16[8,2048]{1,0:T(8,128)(2,1)S(1)}, bf16[8,2048]{1,0:T(8,128)(2,1)S(1)}, u32[]{:S(2)}, u32[]{:S(2)}) collective-permute-start(bf16[8,2048]{1,0:T(8,128)(2,1)S(1)} %collective-permute-done.14), channel_id=1, source_target_pairs={{0,1},{1,2},{2,3},{3,4},{4,5},{5,6},{6,7},{7,8},{8,9},{9,10},{10,1... | collective-permute-start | bytes 98312 | tf_op jit(solution)/shard_map/ppermute | solution.py:116
  142.8 6.0 %collective-permute-start.17 = (bf16[8,2048]{1,0:T(8,128)(2,1)S(1)}, bf16[8,2048]{1,0:T(8,128)(2,1)S(1)}, u32[]{:S(2)}, u32[]{:S(2)}) collective-permute-start(bf16[8,2048]{1,0:T(8,128)(2,1)S(1)} %collective-permute-done.15), channel_id=1, source_target_pairs={{0,15},{1,0},{2,1},{3,2},{4,3},{5,4},{6,5},{7,6},{8,7},{9,8},{10,9... | collective-permute-start | bytes 98312 | tf_op jit(solution)/shard_map/ppermute | solution.py:121
  148.8 6.0 %collective-permute-start.18 = (bf16[8,2048]{1,0:T(8,128)(2,1)S(1)}, bf16[8,2048]{1,0:T(8,128)(2,1)S(1)}, u32[]{:S(2)}, u32[]{:S(2)}) collective-permute-start(bf16[8,2048]{1,0:T(8,128)(2,1)S(1)} %collective-permute-done.16), channel_id=1, source_target_pairs={{0,1},{1,2},{2,3},{3,4},{4,5},{5,6},{6,7},{7,8},{8,9},{9,10},{10,1... | collective-permute-start | bytes 98312 | tf_op jit(solution)/shard_map/ppermute | solution.py:116
  (2 other events, 5.4 us)
